TPU v7x, 256 devices: a whole 4x4x8 slice. The times are simulated.
256 devices in a mesh: ctx: 32 (over x, z), head: 8 (over y, core).
Axes of the slice: x: 4, y: 4, z: 8, core: 2. Of those that a mesh axis runs over, the one named last changes fastest.
Arguments:
- layer_input: bfloat16 [16384, 8192], P('ctx', 'head'), may hold values from -6 to 6
- query_columns: bfloat16 [16384, 8192], P('ctx', 'head'), may hold values from -6 to 6
- key_columns: bfloat16 [16384, 1024], P('ctx', 'head'), may hold values from -6 to 6
- value_columns: bfloat16 [16384, 1024], P('ctx', 'head'), may hold values from -6 to 6
- output_gradient: bfloat16 [16384, 8192], P('ctx', 'head'), may hold values from -6 to 6
Outputs:
- query_grad: bfloat16 [16384, 8192], P('ctx', 'head')
- key_weight_grad: float32 [8192, 1024], P(('head', 'ctx'))
- value_weight_grad: float32 [8192, 1024], P(('head', 'ctx'))
All inputs are finite; a program needn't handle non-finite values.
Results may differ from a plain program's by a relative error of at most 0.014.
Values may be sent and summed in bfloat16 or wider, within the bound.
A program may use at most 128 MiB of HBM per device.

v0:
```python
import jax
import jax.numpy as jnp
from jax import lax
from jax.sharding import PartitionSpec as P

QUERY_HEADS = 64
KEY_VALUE_HEADS = 8
HEAD_SIZE = 128
highest = lax.Precision.HIGHEST


def prefix(value, axis, combine, identity, reverse):
    devices, position = (lax.axis_size(axis), lax.axis_index(axis))
    everything = jax.tree.map(lambda part: lax.all_gather(part, axis), value)
    start = jax.tree.map(
        lambda part, zero: jnp.broadcast_to(jnp.asarray(zero, part.dtype), part.shape),
        value,
        identity,
    )

    def step(k, before):
        at = devices - 1 - k if reverse else k
        reached = at > position if reverse else at < position
        new = combine(before, jax.tree.map(lambda part: part[at], everything))
        return jax.tree.map(lambda a, b: jnp.where(reached, a, b), new, before)

    return lax.fori_loop(0, devices, step, start)


def positive_features(raw):
    wide = raw.astype(jnp.float32)
    return jnp.where(wide > 0, wide + 1.0, jnp.exp(jnp.minimum(wide, 0.0))).astype(jnp.bfloat16)


def feature_derivative(raw):
    wide = raw.astype(jnp.float32)
    return jnp.where(wide > 0, 1.0, jnp.exp(jnp.minimum(wide, 0.0)))


def causal_mask(length):
    rows_at = lax.broadcasted_iota(jnp.int32, (length, length), 0)
    cols_at = lax.broadcasted_iota(jnp.int32, (length, length), 1)
    return cols_at <= rows_at


def block_states(key_features, value_entries):
    states = jnp.einsum(
        "ske,skf->kef", key_features, value_entries, preferred_element_type=jnp.float32
    )
    totals = jnp.sum(key_features.astype(jnp.float32), axis=0)
    return (states, totals)


def block_scores(query_features, key_features):
    attention_scores = jnp.einsum(
        "tkge,ske->kgts", query_features, key_features, preferred_element_type=jnp.float32
    )
    return jnp.where(causal_mask(attention_scores.shape[-1]), attention_scores, jnp.float32(0.0))


def forward_blockwise_pass(
    query_features, value_entries, output_cotangent, prior_state, prior_total, attention_scores
):
    query_wide = query_features.astype(jnp.float32)
    denom = jnp.einsum("tkge,ke->tkg", query_wide, prior_total, precision=highest) + jnp.transpose(
        jnp.sum(attention_scores, axis=-1), (2, 0, 1)
    )
    numer = jnp.einsum("tkge,kef->tkgf", query_wide, prior_state, precision=highest) + jnp.einsum(
        "kgts,skf->tkgf",
        attention_scores.astype(jnp.bfloat16),
        value_entries,
        preferred_element_type=jnp.float32,
    )
    output = numer / denom[..., None]
    wide_cot = output_cotangent.astype(jnp.float32)
    scaled = (wide_cot / denom[..., None]).astype(jnp.bfloat16)
    weight = -jnp.sum(wide_cot * output, axis=-1) / denom
    grad_state = jnp.einsum(
        "tkge,tkgf->kef", query_features, scaled, preferred_element_type=jnp.float32
    )
    grad_total = jnp.einsum("tkge,tkg->ke", query_wide, weight, precision=highest)
    return (scaled, weight, grad_state, grad_total)


def backward_blockwise_pass(
    query_features,
    key_features,
    value_entries,
    lower_triangle_scores,
    scaled,
    weight,
    prior_state,
    prior_total,
    later_state,
    later_total,
):
    dscores = (
        jnp.einsum("tkgf,skf->kgts", scaled, value_entries, preferred_element_type=jnp.float32)
        + jnp.transpose(weight, (1, 2, 0))[..., None]
    )
    dscores = jnp.where(causal_mask(dscores.shape[-1]), dscores, jnp.float32(0.0)).astype(
        jnp.bfloat16
    )
    grad_query = (
        jnp.einsum("tkgf,kef->tkge", scaled.astype(jnp.float32), prior_state, precision=highest)
        + weight[..., None] * prior_total[None, :, None, :]
        + jnp.einsum("kgts,ske->tkge", dscores, key_features, preferred_element_type=jnp.float32)
    )
    key_gradient_rows = (
        jnp.einsum("kgts,tkge->ske", dscores, query_features, preferred_element_type=jnp.float32)
        + jnp.einsum(
            "kef,skf->ske", later_state, value_entries.astype(jnp.float32), precision=highest
        )
        + later_total[None]
    )
    value_gradient_rows = jnp.einsum(
        "kgts,tkgf->skf", lower_triangle_scores, scaled, preferred_element_type=jnp.float32
    ) + jnp.einsum("kef,ske->skf", later_state, key_features.astype(jnp.float32), precision=highest)
    return (grad_query, key_gradient_rows, value_gradient_rows)


def add_pair(earlier, later):
    return (earlier[0] + later[0], earlier[1] + later[1])


def shards(layer_input, query_columns, key_columns, value_columns, output_gradient):
    rows = query_columns.shape[0]
    local_kv = key_columns.shape[1] // HEAD_SIZE
    query_group_count = QUERY_HEADS // KEY_VALUE_HEADS
    block = min(256, rows)
    count = rows // block
    query_features = positive_features(query_columns).reshape(
        count, block, local_kv, query_group_count, HEAD_SIZE
    )
    key_features = positive_features(key_columns).reshape(count, block, local_kv, HEAD_SIZE)
    value_entries = value_columns.reshape(count, block, local_kv, HEAD_SIZE)
    output_cotangent = output_gradient.reshape(count, block, local_kv, query_group_count, HEAD_SIZE)
    pieces = [block_states(key_features[index], value_entries[index]) for index in range(count)]
    dev_state = pieces[0][0]
    dev_total = pieces[0][1]
    index = 1
    dev_state = dev_state + pieces[index][0]
    dev_total = dev_total + pieces[index][1]
    empty = (jnp.zeros_like(dev_state), jnp.zeros_like(dev_total))
    before_state, before_total = prefix((dev_state, dev_total), "ctx", add_pair, empty, False)
    priors = []
    running_state, running_total = (before_state, before_total)
    for index in range(count):
        priors.append((running_state, running_total))
        running_state = running_state + pieces[index][0]
        running_total = running_total + pieces[index][1]
    forwards = []
    for index in range(count):
        attention_scores = block_scores(query_features[index], key_features[index])
        forwards.append(
            forward_blockwise_pass(
                query_features[index],
                value_entries[index],
                output_cotangent[index],
                priors[index][0],
                priors[index][1],
                attention_scores,
            )
        )
    dev_gstate = forwards[0][2]
    dev_gtotal = forwards[0][3]
    index = 1
    dev_gstate = dev_gstate + forwards[index][2]
    dev_gtotal = dev_gtotal + forwards[index][3]
    after_state, after_total = prefix((dev_gstate, dev_gtotal), "ctx", add_pair, empty, True)
    laters = [None] * count
    running_state, running_total = (after_state, after_total)
    for index in range(count - 1, -1, -1):
        laters[index] = (running_state, running_total)
        running_state = running_state + forwards[index][2]
        running_total = running_total + forwards[index][3]
    query_parts = []
    key_parts = []
    value_parts = []
    for index in range(count):
        lower_triangle_scores = block_scores(query_features[index], key_features[index]).astype(
            jnp.bfloat16
        )
        grad_query, key_gradient_rows, value_gradient_rows = backward_blockwise_pass(
            query_features[index],
            key_features[index],
            value_entries[index],
            lower_triangle_scores,
            forwards[index][0],
            forwards[index][1],
            priors[index][0],
            priors[index][1],
            laters[index][0],
            laters[index][1],
        )
        query_parts.append(grad_query)
        key_parts.append(key_gradient_rows)
        value_parts.append(value_gradient_rows)
    query_grad = (
        jnp.concatenate(query_parts, axis=0).reshape(rows, query_columns.shape[1])
        * feature_derivative(query_columns)
    ).astype(jnp.bfloat16)
    key_gradient = (
        jnp.concatenate(key_parts, axis=0).reshape(rows, key_columns.shape[1])
        * feature_derivative(key_columns)
    ).astype(jnp.bfloat16)
    value_gradient = (
        jnp.concatenate(value_parts, axis=0)
        .reshape(rows, value_columns.shape[1])
        .astype(jnp.bfloat16)
    )
    key_all, value_all = (
        lax.all_gather(key_gradient, "head", axis=1, tiled=True),
        lax.all_gather(value_gradient, "head", axis=1, tiled=True),
    )
    joined = jnp.concatenate([key_all, value_all], axis=1)
    summed = lax.psum_scatter(
        jnp.einsum("tr,tc->rc", layer_input, joined, preferred_element_type=jnp.float32),
        "ctx",
        scatter_dimension=0,
        tiled=True,
    )
    half_width = key_all.shape[1]
    return (query_grad, summed[:, :half_width], summed[:, half_width:])


def solution(mesh):
    placed = (
        P("ctx", "head"),
        P("ctx", "head"),
        P("ctx", "head"),
        P("ctx", "head"),
        P("ctx", "head"),
    )
    return jax.shard_map(
        shards,
        mesh=mesh,
        in_specs=placed,
        out_specs=(P("ctx", "head"), P(("head", "ctx"), None), P(("head", "ctx"), None)),
        check_vma=False,
    )
```

profile of v0, /device:TPU:8, one launch (start us, length us, event | category | flops | bytes accessed | tf_op | source)
XLA Modules:
  0.0 587.1 jit_solution(2239093417903597590)
XLA Ops:
  9.3 1.7 convolution_add_fusion
  11.1 1.5 copy.102
  12.7 2.8 slice_convert_fusion.1
  15.5 2.5 copy.106
  18.0 1.3 copy.118
  19.4 41.8 %all-gather.5 = f32[32,1,128]{2,1,0:T(1,128)S(1)} all-gather(f32[1,1,128]{2,1,0:T(1,128)S(1)} %add_bitcast_fusion), channel_id=3, replica_groups=mesh['ctx'=32,'head'=8] {'ctx'}, dimensions={0}, use_global_device_ids=true | all-gather | bytes 16896 | tf_op jit(solution)/shard_map/all_gather | solution.py:14
  63.0 1.5 fusion.14
  64.5 27.5 %all-gather.14.cloned.1.call-done = f32[4096,128]{1,0:T(8,128)} async-done(((f32[128,128]{1,0:T(8,128)}), f32[4096,128]{1,0:T(8,128)}) %all-gather.14.cloned.1.call-update) | async-done | bytes 2097168 | tf_op jit(solution)/shard_map/all_gather | solution.py:14
  92.0 28.9 %while.34 = (s32[]{:T(128)}, f32[1,128,128]{2,1,0:T(8,128)S(1)}, f32[1,128]{1,0:T(1,128)S(1)}, s32[]{:T(128)}, f32[32,1,128,128]{3,2,1,0:T(8,128)}, /*index=5*/f32[32,1,128]{2,1,0:T(1,128)S(1)}, s32[]{:T(128)}, s32[]{:T(128)}) while((s32[]{:T(128)}, f32[1,128,128]{2,1,0:T(8,128)S(1)}, f32[1,128]{1,0:T(1,128)S(1)}, s32[]{:T(128)}, ...), condition=%wide.region_3.4_spmd.clone, body=%wide.region_2.3_spmd.clone.sunk | while | flops 49540 | bytes 198267 | solution.py:27
  120.9 2.7 fusion.105
  123.6 2.7 fusion.107
  126.3 1.5 copy.154
  127.9 1.6 copy.145
  129.5 1.4 divide_convert_fusion
  131.7 1.3 fusion.117
  134.2 2.6 convolution_bitcast_fusion.6
  136.8 1.4 convolution_bitcast_fusion.5
  139.2 2.6 copy.181
  142.8 2.6 copy.177
  145.4 2.5 fusion.30
  149.8 39.3 %all-gather.6 = f32[32,1,128]{2,1,0:T(1,128)} all-gather(f32[1,1,128]{2,1,0:T(1,128)S(1)} %fusion.41), channel_id=5, replica_groups=mesh['ctx'=32,'head'=8] {'ctx'}, dimensions={0}, use_global_device_ids=true | all-gather | bytes 16896 | tf_op jit(solution)/shard_map/all_gather | solution.py:14
  189.2 20.2 %all-gather.16.cloned.1.call-done = f32[4096,128]{1,0:T(8,128)} async-done(((f32[128,128]{1,0:T(8,128)}), f32[4096,128]{1,0:T(8,128)}) %all-gather.16.cloned.1.call-update) | async-done | bytes 2097168 | tf_op jit(solution)/shard_map/all_gather | solution.py:14
  209.4 66.8 %while.35 = (s32[]{:T(128)}, f32[1,128,128]{2,1,0:T(8,128)S(1)}, f32[1,128]{1,0:T(1,128)}, s32[]{:T(128)}, f32[32,1,128,128]{3,2,1,0:T(8,128)}, /*index=5*/f32[3...) while((s32[]{:T(128)}, f32[1,128,128]{2,1,0:T(8,128)S(1)}, f32[1,128]{1,0:T(1,128)}, ...), condition=%wide.region_9.10_spmd.clone, body=%wide.region_8.9_spmd.clone.sunk | while | flops 49544 | bytes 198329 | solution.py:27
  215.6 1.2 broadcast_select_fusion.7
  219.8 1.2 broadcast_select_fusion.7
  221.9 1.2 broadcast_select_fusion.7
  228.1 1.2 broadcast_select_fusion.7
  230.2 1.2 broadcast_select_fusion.7
  234.4 1.2 broadcast_select_fusion.7
  244.8 1.2 broadcast_select_fusion.7
  246.9 1.2 broadcast_select_fusion.7
  249.0 1.2 broadcast_select_fusion.7
  251.1 1.2 broadcast_select_fusion.7
  257.4 1.2 broadcast_select_fusion.7
  259.5 1.2 broadcast_select_fusion.7
  269.9 1.2 broadcast_select_fusion.7
  272.0 1.2 broadcast_select_fusion.7
  276.6 1.7 fusion.38
  279.9 1.6 fusion.48
  284.8 17.6 %all-gather.18.cloned.1.call-done = bf16[512,1,1024]{2,0,1:T(8,128)(2,1)} async-done(((bf16[512,1,128]{2,0,1:T(8,128)(2,1)}), bf16[512,1,1024]{2,0,1:T(8,128)(2,1)}) %all-gather.18.cloned.1.call-update) | async-done | bytes 1048592 | tf_op jit(solution)/shard_map/all_gather | solution.py:214
  302.4 29.2 %all-gather.12.cloned.1.call-done = bf16[512,1024]{1,0:T(8,128)(2,1)} async-done(((bf16[512,128]{1,0:T(8,128)(2,1)}), bf16[512,1024]{1,0:T(8,128)(2,1)}) %all-gather.12.cloned.1.call-update) | async-done | bytes 1048592 | tf_op jit(solution)/shard_map/all_gather | solution.py:213
  331.6 7.2 %convolution_bitcast_fusion = f32[1024,2048]{0,1:T(8,128)} fusion(bf16[512,1024]{1,0:T(8,128)(2,1)S(1)} %copy-done, bf16[512,1024]{1,0:T(8,128)(2,1)} %bitcast.434, bf16[512,1024]{1,0:T(8,128)(2,1)} %all-gather.12.cloned.1.call-done), kind=kOutput, calls=%fused_computation.6 | convolution fusion | flops 2151677952 | bytes 11534336 | tf_op jit(solution)/shard_map/tr,tc->rc/dot_general | solution.py:218
  338.8 9.2 %copy.191 = f32[1024,2048]{1,0:T(8,128)} copy(f32[1024,2048]{0,1:T(8,128)} %convolution_bitcast_fusion) | data formatting | bytes 16777216
  348.0 1.2 copy-done.14
  352.9 1.5 fusion.5
  354.4 2.3 copy.142
  356.6 222.3 %reduce-scatter.4.cloned.1.call-done = f32[32,2048]{1,0:T(8,128)} async-done(((f32[1024,2048]{1,0:T(8,128)}), f32[32,2048]{1,0:T(8,128)}) %reduce-scatter.4.cloned.1.call-update) | async-done | bytes 262160
  578.9 1.7 fusion.116
  (256 shorter events, 95.3 us)
Async XLA Ops:
  7.2 324.5 %copy-start = (bf16[512,1024]{1,0:T(8,128)(2,1)S(1)}, bf16[512,1024]{1,0:T(8,128)(2,1)}, u32[]{:S(2)}) copy-start(bf16[512,1024]{1,0:T(8,128)(2,1)} %param.9) | copy-start | bytes 3145732
  7.2 84.8 %all-gather.14.cloned.1.call-start = ((), (), s32[]{:S(2)}) async-start(), calls=%async_computation.2 | async-start | bytes 2162688 | tf_op jit(solution)/shard_map/all_gather | solution.py:14
  9.3 1.8 copy-start.26
  11.1 198.3 %all-gather.16.cloned.1.call-start = ((), (), s32[]{:S(2)}) async-start(), calls=%async_computation.3 | async-start | bytes 2162688 | tf_op jit(solution)/shard_map/all_gather | solution.py:14
  12.6 48.6 %copy-start.8 = (bf16[512,1024]{0,1:T(8,128)(2,1)}, bf16[512,1024]{0,1:T(8,128)(2,1)S(1)}, u32[]{:S(2)}) copy-start(bf16[512,1024]{0,1:T(8,128)(2,1)S(1)} %copy.102) | copy-start | bytes 3145732
  19.4 101.5 %copy-start.43 = (f32[128]{0:T(128)}, f32[128]{0:T(128)S(1)}, u32[]{:S(2)}) copy-start(f32[128]{0:T(128)S(1)} %get-tuple-element.360) | copy-start | bytes 1540
  61.8 0.8 copy-start.1
  61.8 1.2 copy-start.4
  64.5 64.9 %copy-start.32 = (f32[8,256]{1,0:T(8,128)}, f32[8,256]{1,0:T(8,128)S(1)}, u32[]{:S(2)}) copy-start(f32[8,256]{1,0:T(8,128)S(1)} %get-tuple-element.362) | copy-start | bytes 24580
  64.5 68.5 %copy-start.30 = (f32[8,256]{1,0:T(8,128)}, f32[8,256]{1,0:T(8,128)S(1)}, u32[]{:S(2)}) copy-start(f32[8,256]{1,0:T(8,128)S(1)} %get-tuple-element.361) | copy-start | bytes 24580
  120.9 2.7 copy-start.40
  127.9 6.2 %copy-start.34 = (f32[1,256,8]{1,2,0:T(8,128)}, f32[1,256,8]{1,2,0:T(8,128)S(1)}, u32[]{:S(2)}) copy-start(f32[1,256,8]{1,2,0:T(8,128)S(1)} %copy.154) | copy-start | bytes 24580
  129.4 4.6 copy-start.36
  129.4 3.7 copy-start.5
  129.5 3.7 copy-start.24
  130.9 0.8 copy-start.10
  133.1 12.3 %copy-start.38 = (f32[256,8]{0,1:T(8,128)}, f32[256,8]{0,1:T(8,128)S(1)}, u32[]{:S(2)}) copy-start(f32[256,8]{0,1:T(8,128)S(1)} %fusion.102) | copy-start | bytes 24580
  134.1 168.3 %all-gather.18.cloned.1.call-start = ((), (), s32[]{:S(2)}) async-start(), calls=%async_computation.4 | async-start | bytes 1179648 | tf_op jit(solution)/shard_map/all_gather | solution.py:214
  134.2 2.6 copy-start.21
  145.4 2.6 copy-start.2
  145.4 2.6 copy-start.12
  145.4 2.6 copy-start.23
  145.4 2.6 copy-start.27
  148.0 0.8 copy-start.31
  148.0 0.8 copy-start.33
  148.0 0.8 copy-start.35
  148.0 1.3 copy-start.6
  276.2 2.1 copy-start.15
  276.2 2.1 copy-start.25
  276.2 2.1 copy-start.39
  278.3 1.4 copy-start.11
  278.3 1.6 copy-start.16
  279.5 52.1 %all-gather.12.cloned.1.call-start = ((), (), s32[]{:S(2)}) async-start(), calls=%async_computation.1 | async-start | bytes 1179648 | tf_op jit(solution)/shard_map/all_gather | solution.py:213
  279.9 1.6 copy-start.22
  281.5 1.0 copy-start.17
  281.5 1.0 copy-start.19
  281.6 1.5 copy-start.42
  281.6 1.5 copy-start.46
  281.6 1.5 copy-start.7
  282.0 1.5 copy-start.13
  282.1 1.5 copy-start.3
  282.5 1.4 copy-start.29
  284.7 294.2 %reduce-scatter.4.cloned.1.call-start = ((), (), s32[]{:S(2)}) async-start(), calls=%async_computation.5 | async-start | bytes 8650752
  348.0 1.2 copy-start.14
  349.2 1.0 copy-start.20
  349.6 1.4 copy-start.18
  349.6 1.4 copy-start.28
  351.6 1.2 copy-start.9
  (4 other events, 2.7 us)
Sparse Core Ops, SparseCore 0:
  11.2 80.7 all-gather.13
  134.2 75.1 all-gather.15
  279.6 22.7 all-gather.17
  304.7 26.9 all-gather.11
  348.1 230.7 reduce-scatter.3
where the time goes:
time: 591 us; the launch traced here: 587 us
  waiting for transfers between devices  317 us (54%)
  other arithmetic  105 us (18%)
  blocking collectives  81.1 us (14%)
  matrix products  34.4 us (6%)
  local copies, waits for them, and re-layouts  33.4 us (6%)
  between operations  14.6 us (2%)
    unnamed x6, waiting for transfers between devices  222 us
    select_n x128, other arithmetic, step(): return jax.tree.map(lambda a, b: jnp.where(reached, a, b), new, before)  93.9 us
    all_gather x2, blocking collectives, prefix(): everything = jax.tree.map(lambda part: lax.all_gather(part, axis), value)  81.1 us
    all_gather x2, waiting for transfers between devices, prefix(): everything = jax.tree.map(lambda part: lax.all_gather(part, axis), value)  47.7 us
    all_gather x1, waiting for transfers between devices, shards(): lax.all_gather(key_gradient, 'head', axis=1, tiled=True)  29.2 us
    all_gather x1, waiting for transfers between devices, shards(): lax.all_gather(value_gradient, 'head', axis=1, tiled=True)  17.6 us
    unnamed x97, local copies, waits for them, and re-layouts  17.5 us
  transfers between devices with their start and end apart: 5, of which 5 were waited for; matrix products, arithmetic and copies ran while one was open for 6% of the time, Pallas kernels for 0%

commit v1 on v0

--- a/solution.py
+++ b/solution.py
@@ -7,6 +7,13 @@
 KEY_VALUE_HEADS = 8
 HEAD_SIZE = 128
 highest = lax.Precision.HIGHEST
+
+
+def gather_over(x, axis, d):
+    devices = lax.axis_size(axis)
+    blocks = jnp.stack([x for _ in range(devices)])
+    blocks = lax.all_to_all(blocks, axis, split_axis=0, concat_axis=0)
+    return jnp.concatenate(blocks, axis=d)
 
 
 def prefix(value, axis, combine, identity, reverse):
@@ -210,7 +217,7 @@
         .astype(jnp.bfloat16)
     )
     key_all, value_all = (
-        lax.all_gather(key_gradient, "head", axis=1, tiled=True),
+        gather_over(key_gradient, "head", 1),
         lax.all_gather(value_gradient, "head", axis=1, tiled=True),
     )
     joined = jnp.concatenate([key_all, value_all], axis=1)

time: 591 us -> 566 us (0.958)
  waiting for transfers between devices: 317 us -> 263 us
  blocking collectives: 81.1 us -> 105 us
    all_gather x1 -> x0, waiting for transfers between devices: 29.2 us -> none  [shards(): lax.all_gather(key_gradient, 'head', axis=1, tiled=True)]
    all_to_all x0 -> x1, blocking collectives: none -> 23.5 us  [gather_over(): blocks = lax.all_to_all(blocks, axis, split_axis=0, concat_axis=0)]
    all_gather x1, waiting for transfers between devices: 17.6 us -> 0.01 us  [shards(): lax.all_gather(value_gradient, 'head', axis=1, tiled=True)]
    unnamed x6 -> x5, waiting for transfers between devices: 222 us -> 219 us
  transfers between devices with their start and end apart: 5 -> 4, of which waited for: 5 -> 3; matrix products, arithmetic and copies ran while one was open for 6% -> 7% of each run, Pallas kernels for 0% -> 0%
where the time goes in v1:
time: 566 us; the launch traced here: 562 us
  waiting for transfers between devices  263 us (46%)
  blocking collectives  105 us (19%)
  other arithmetic  104 us (18%)
  matrix products  39.4 us (7%)
  local copies, waits for them, and re-layouts  34.1 us (6%)
  between operations  14.6 us (3%)
    unnamed x5, waiting for transfers between devices  219 us
    select_n x128, other arithmetic, step(): return jax.tree.map(lambda a, b: jnp.where(reached, a, b), new, before)  93.9 us
    all_gather x2, blocking collectives, prefix(): everything = jax.tree.map(lambda part: lax.all_gather(part, axis), value)  81.2 us
    all_gather x2, waiting for transfers between devices, prefix(): everything = jax.tree.map(lambda part: lax.all_gather(part, axis), value)  43.4 us
    all_to_all x1, blocking collectives, gather_over(): blocks = lax.all_to_all(blocks, axis, split_axis=0, concat_axis=0)  23.5 us
    unnamed x97, local copies, waits for them, and re-layouts  18.1 us
  transfers between devices with their start and end apart: 4, of which 3 were waited for; matrix products, arithmetic and copies ran while one was open for 7% of the time, Pallas kernels for 0%

profile of v1, /device:TPU:8, one launch (start us, length us, event | category | flops | bytes accessed | tf_op | source)
XLA Modules:
  0.0 561.7 jit_solution(15373087524890025800)
XLA Ops:
  9.3 1.7 convolution_add_fusion
  11.1 1.5 copy.104
  12.7 2.8 slice_convert_fusion.1
  15.5 2.5 copy.108
  18.0 1.3 copy.120
  19.4 41.8 %all-gather.5 = f32[32,1,128]{2,1,0:T(1,128)S(1)} all-gather(f32[1,1,128]{2,1,0:T(1,128)S(1)} %add_bitcast_fusion), channel_id=3, replica_groups=mesh['ctx'=32,'head'=8] {'ctx'}, dimensions={0}, use_global_device_ids=true | all-gather | bytes 16896 | tf_op jit(solution)/shard_map/all_gather | solution.py:21
  63.0 1.5 fusion.14
  64.5 27.5 %all-gather.11.cloned.1.call-done = f32[4096,128]{1,0:T(8,128)} async-done(((f32[128,128]{1,0:T(8,128)}), f32[4096,128]{1,0:T(8,128)}) %all-gather.11.cloned.1.call-update) | async-done | bytes 2097168 | tf_op jit(solution)/shard_map/all_gather | solution.py:21
  92.0 28.9 %while.34 = (s32[]{:T(128)}, f32[1,128,128]{2,1,0:T(8,128)S(1)}, f32[1,128]{1,0:T(1,128)S(1)}, s32[]{:T(128)}, f32[32,1,128,128]{3,2,1,0:T(8,128)}, /*index=5*/f32[32,1,128]{2,1,0:T(1,128)S(1)}, s32[]{:T(128)}, s32[]{:T(128)}) while((s32[]{:T(128)}, f32[1,128,128]{2,1,0:T(8,128)S(1)}, f32[1,128]{1,0:T(1,128)S(1)}, s32[]{:T(128)}, ...), condition=%wide.region_3.4_spmd.clone, body=%wide.region_2.3_spmd.clone.sunk | while | flops 49540 | bytes 198267 | solution.py:34
  120.9 2.7 fusion.105
  123.6 2.7 fusion.107
  126.3 1.5 copy.157
  127.9 1.6 copy.148
  129.5 1.4 divide_convert_fusion
  131.7 1.3 fusion.117
  134.2 2.6 convolution_bitcast_fusion.6
  136.8 1.4 convolution_bitcast_fusion.5
  139.2 2.5 copy.184
  142.8 2.5 copy.180
  145.3 2.5 fusion.30
  149.9 39.5 %all-gather.6 = f32[32,1,128]{2,1,0:T(1,128)} all-gather(f32[1,1,128]{2,1,0:T(1,128)S(1)} %fusion.41), channel_id=5, replica_groups=mesh['ctx'=32,'head'=8] {'ctx'}, dimensions={0}, use_global_device_ids=true | all-gather | bytes 16896 | tf_op jit(solution)/shard_map/all_gather | solution.py:21
  190.5 1.4 fusion.17
  192.0 1.4 fusion.18
  193.4 16.0 %all-gather.13.cloned.1.call-done = f32[4096,128]{1,0:T(8,128)} async-done(((f32[128,128]{1,0:T(8,128)}), f32[4096,128]{1,0:T(8,128)}) %all-gather.13.cloned.1.call-update) | async-done | bytes 2097168 | tf_op jit(solution)/shard_map/all_gather | solution.py:21
  209.4 66.8 %while.35 = (s32[]{:T(128)}, f32[1,128,128]{2,1,0:T(8,128)S(1)}, f32[1,128]{1,0:T(1,128)}, s32[]{:T(128)}, f32[32,1,128,128]{3,2,1,0:T(8,128)}, /*index=5*/f32[3...) while((s32[]{:T(128)}, f32[1,128,128]{2,1,0:T(8,128)S(1)}, f32[1,128]{1,0:T(1,128)}, ...), condition=%wide.region_9.10_spmd.clone, body=%wide.region_8.9_spmd.clone.sunk | while | flops 49544 | bytes 198329 | solution.py:34
  211.4 1.2 broadcast_select_fusion.7
  213.5 1.2 broadcast_select_fusion.7
  215.6 1.2 broadcast_select_fusion.7
  224.0 1.2 broadcast_select_fusion.7
  226.1 1.2 broadcast_select_fusion.7
  228.2 1.2 broadcast_select_fusion.7
  232.4 1.2 broadcast_select_fusion.7
  242.8 1.2 broadcast_select_fusion.7
  249.1 1.2 broadcast_select_fusion.7
  253.2 1.2 broadcast_select_fusion.7
  255.3 1.2 broadcast_select_fusion.7
  269.9 1.2 broadcast_select_fusion.7
  274.1 1.2 broadcast_select_fusion.7
  276.7 1.3 fusion.104
  278.1 1.5 fusion.38
  283.3 1.7 fusion.36
  285.7 23.5 %all_to_all.5 = bf16[8,512,128]{1,2,0:T(8,128)(2,1)} all-to-all(bf16[8,512,128]{1,2,0:T(8,128)(2,1)S(1)} %stack.2), channel_id=1, replica_groups=mesh['ctx'=32,'head'=8] {'head'}, dimensions={0} | all-to-all | bytes 2097152 | tf_op jit(solution)/shard_map/all_to_all | solution.py:15
  309.2 7.1 %convolution_bitcast_fusion = f32[1024,2048]{0,1:T(8,128)} fusion(bf16[512,1024]{1,0:T(8,128)(2,1)S(1)} %copy-done, bf16[512,1024]{0,1:T(8,128)(2,1)} %bitcast.438, bf16[512,1024]{0,1:T(8,128)(2,1)} %bitcast.427), kind=kOutput, calls=%fused_computation.6 | convolution fusion | flops 2151677952 | bytes 11534336 | tf_op jit(solution)/shard_map/tr,tc->rc/dot_general | solution.py:225
  316.4 9.2 %copy.192 = f32[1024,2048]{1,0:T(8,128)} copy(f32[1024,2048]{0,1:T(8,128)} %convolution_bitcast_fusion) | data formatting | bytes 16777216
  330.4 1.5 fusion.5
  331.9 2.3 copy.145
  334.2 219.2 %reduce-scatter.4.cloned.1.call-done = f32[32,2048]{1,0:T(8,128)} async-done(((f32[1024,2048]{1,0:T(8,128)}), f32[32,2048]{1,0:T(8,128)}) %reduce-scatter.4.cloned.1.call-update) | async-done | bytes 262160
  553.4 1.7 fusion.116
  (256 shorter events, 98.6 us)
Async XLA Ops:
  7.2 302.1 %copy-start = (bf16[512,1024]{1,0:T(8,128)(2,1)S(1)}, bf16[512,1024]{1,0:T(8,128)(2,1)}, u32[]{:S(2)}) copy-start(bf16[512,1024]{1,0:T(8,128)(2,1)} %param.9) | copy-start | bytes 3145732
  7.2 84.8 %all-gather.11.cloned.1.call-start = ((), (), s32[]{:S(2)}) async-start(), calls=%async_computation.2 | async-start | bytes 2162688 | tf_op jit(solution)/shard_map/all_gather | solution.py:21
  9.3 1.8 copy-start.27
  11.1 198.3 %all-gather.13.cloned.1.call-start = ((), (), s32[]{:S(2)}) async-start(), calls=%async_computation.3 | async-start | bytes 2162688 | tf_op jit(solution)/shard_map/all_gather | solution.py:21
  12.6 48.6 %copy-start.8 = (bf16[512,1024]{0,1:T(8,128)(2,1)}, bf16[512,1024]{0,1:T(8,128)(2,1)S(1)}, u32[]{:S(2)}) copy-start(bf16[512,1024]{0,1:T(8,128)(2,1)S(1)} %copy.104) | copy-start | bytes 3145732
  19.4 101.5 %copy-start.44 = (f32[128]{0:T(128)}, f32[128]{0:T(128)S(1)}, u32[]{:S(2)}) copy-start(f32[128]{0:T(128)S(1)} %get-tuple-element.360) | copy-start | bytes 1540
  61.8 0.8 copy-start.1
  61.8 1.2 copy-start.4
  64.5 65.0 %copy-start.33 = (f32[8,256]{1,0:T(8,128)}, f32[8,256]{1,0:T(8,128)S(1)}, u32[]{:S(2)}) copy-start(f32[8,256]{1,0:T(8,128)S(1)} %get-tuple-element.362) | copy-start | bytes 24580
  64.5 68.5 %copy-start.31 = (f32[8,256]{1,0:T(8,128)}, f32[8,256]{1,0:T(8,128)S(1)}, u32[]{:S(2)}) copy-start(f32[8,256]{1,0:T(8,128)S(1)} %get-tuple-element.361) | copy-start | bytes 24580
  120.9 2.7 copy-start.41
  127.9 6.2 %copy-start.35 = (f32[1,256,8]{1,2,0:T(8,128)}, f32[1,256,8]{1,2,0:T(8,128)S(1)}, u32[]{:S(2)}) copy-start(f32[1,256,8]{1,2,0:T(8,128)S(1)} %copy.157) | copy-start | bytes 24580
  129.5 4.6 copy-start.37
  129.5 3.6 copy-start.5
  129.5 3.6 copy-start.25
  130.9 0.8 copy-start.10
  133.1 12.2 %copy-start.39 = (f32[256,8]{0,1:T(8,128)}, f32[256,8]{0,1:T(8,128)S(1)}, u32[]{:S(2)}) copy-start(f32[256,8]{0,1:T(8,128)S(1)} %fusion.102) | copy-start | bytes 24580
  134.1 175.1 %all-gather.15.cloned.1.call-start = ((), (), s32[]{:S(2)}) async-start(), calls=%async_computation.4 | async-start | bytes 1179648 | tf_op jit(solution)/shard_map/all_gather | solution.py:221
  134.2 2.6 copy-start.22
  145.3 2.6 copy-start.2
  145.3 2.6 copy-start.14
  145.3 2.6 copy-start.24
  145.3 2.6 copy-start.28
  147.9 0.8 copy-start.32
  147.9 0.8 copy-start.34
  147.9 0.8 copy-start.36
  147.9 0.8 copy-start.38
  148.0 1.3 copy-start.6
  148.0 41.4 %copy-start.11 = (bf16[512,1024]{1,0:T(8,128)(2,1)S(1)}, bf16[512,1024]{1,0:T(8,128)(2,1)}, u32[]{:S(2)}) copy-start(bf16[512,1024]{1,0:T(8,128)(2,1)} %param.13) | copy-start | bytes 3145732
  148.0 41.4 %copy-start.16 = (f32[256,1024]{1,0:T(8,128)S(1)}, f32[256,1024]{1,0:T(8,128)}, u32[]{:S(2)}) copy-start(f32[256,1024]{1,0:T(8,128)} %copy.184) | copy-start | bytes 3145732
  148.0 41.4 %copy-start.17 = (f32[256,1024]{1,0:T(8,128)S(1)}, f32[256,1024]{1,0:T(8,128)}, u32[]{:S(2)}) copy-start(f32[256,1024]{1,0:T(8,128)} %copy.180) | copy-start | bytes 3145732
  189.3 1.2 copy-start.23
  189.7 0.8 copy-start.20
  189.7 2.3 copy-start.18
  276.2 3.4 copy-start.15
  276.2 3.4 copy-start.26
  276.2 3.4 copy-start.40
  279.6 3.7 copy-start.7
  280.1 4.8 copy-start.3
  280.1 4.8 copy-start.12
  280.1 4.8 copy-start.43
  280.8 272.6 %reduce-scatter.4.cloned.1.call-start = ((), (), s32[]{:S(2)}) async-start(), calls=%async_computation.5 | async-start | bytes 8650752
  281.1 4.4 copy-start.30
  325.6 1.2 copy-start.13
  326.8 1.0 copy-start.21
  327.1 1.4 copy-start.19
  327.1 1.4 copy-start.29
  329.2 1.2 copy-start.9
  (3 other events, 2.0 us)
Sparse Core Ops, SparseCore 0:
  11.2 80.7 all-gather.10
  134.2 75.1 all-gather.12
  281.0 25.8 all-gather.14
  325.7 227.6 reduce-scatter.3
